TPU v7x, 256 devices: a whole 4x4x8 slice. The times are simulated.
256 devices in a mesh: blk: 32 (over z, x), span: 8 (over y, core).
Axes of the slice: x: 4, y: 4, z: 8, core: 2. Of those that a mesh axis runs over, the one named last changes fastest.
Arguments:
- fluid_adjoint_in: float32 [5, 256, 256, 128], P(None, 'blk', 'span'), may hold values from -4 to 4
- fluid_source: float32 [5, 256, 256, 128], P(None, 'blk', 'span'), may hold values from -24 to 24
- velocity: float32 [3, 256, 256, 128], P(None, 'blk', 'span'), may hold values from 0.1 to 1
- diffusion: float32 [5], replicated, may hold values from 0.5 to 2
- jacobian: float32 [5, 5], replicated, may hold values from -0.4 to 0.4
- wall_coefficient: float32 [32, 256, 128], P('blk', 'span'), may hold values from 0.5 to 2
- metal_costate_prior: float32 [512, 256, 128], P('blk', 'span'), may hold values from -4 to 4
- solid_source: float32 [512, 256, 128], P('blk', 'span'), may hold values from -12 to 12
- conductivity: float32 [512, 256, 128], P('blk', 'span'), may hold values from 0.3 to 3
- tile_owner: int32 [8, 1024, 1], P('span', 'blk'), may hold values from 0 to 31; in each aligned block of 32 rows (0 to 31, 32 to 63, ..., all dimensions but the last counted through in order) at most 3 rows name the same one
- tile_target: int32 [8, 1024], P('span', 'blk'), may hold values from 0 to 31
Outputs:
- fluid_adjoint: float32 [5, 256, 256, 128], P(None, 'blk', 'span')
- solid_adjoint: float32 [512, 256, 128], P('blk', 'span')
- residual_norms: float32 [6], replicated
Inputs may be any that keep to these rules, and one draw needn't show every extreme that they name: `tile_owner`: within the 32 wall tiles of one fluid block (the rows of one device), no owner is named more than 3 times, a bound that some block reaches; every owner is named by some tile.
All inputs are finite; a program needn't handle non-finite values.
Results may differ from a plain program's by a relative error of at most 0.004.
Values sent between devices are 32-bit elements; how exact they have to be, the bound alone decides.
A program may use at most 64 MiB of HBM per device.

v0:
```python
import jax
import jax.numpy as jnp
from jax import lax
from jax.sharding import PartitionSpec as P

FSWEEPS = 4
SSWEEPS = 4
damping_weight = 0.8


def padded(block, sides, width):
    for axis, dim in sides:
        count = lax.axis_size(axis)
        forward = [(i, i + 1) for i in range(count - 1)]
        backward = [(target, source) for source, target in forward]
        low = lax.ppermute(
            lax.slice_in_dim(block, block.shape[dim] - width, None, axis=dim), axis, forward
        )
        high = lax.ppermute(lax.slice_in_dim(block, 0, width, axis=dim), axis, backward)
        block = jnp.concatenate([low, block, high], axis=dim)
    return block


def fluid_operator(bordered_grid_data, velocity, spread, jacobian):
    centre = bordered_grid_data[:, 1:-1, 1:-1, 1:-1]
    x_next = bordered_grid_data[:, 2:, 1:-1, 1:-1]
    y_next = bordered_grid_data[:, 1:-1, 2:, 1:-1]
    z_next = bordered_grid_data[:, 1:-1, 1:-1, 2:]
    beside_all = (
        x_next
        + bordered_grid_data[:, :-2, 1:-1, 1:-1]
        + y_next
        + bordered_grid_data[:, 1:-1, :-2, 1:-1]
        + z_next
        + bordered_grid_data[:, 1:-1, 1:-1, :-2]
    )
    mixing = jnp.einsum("fg,gxyz->fxyz", jacobian, centre, precision=lax.Precision.HIGHEST)
    velocity_sum = velocity[0] + velocity[1] + velocity[2]
    return (
        (6.0 * spread + velocity_sum) * centre
        - spread * beside_all
        - velocity[0] * x_next
        - velocity[1] * y_next
        - velocity[2] * z_next
        + mixing
    )


def face_conductance(kappa_rim):
    centre = kappa_rim[1:-1, 1:-1, 1:-1]
    return (
        0.5 * (centre + kappa_rim[2:, 1:-1, 1:-1]),
        0.5 * (centre + kappa_rim[:-2, 1:-1, 1:-1]),
        0.5 * (centre + kappa_rim[1:-1, 2:, 1:-1]),
        0.5 * (centre + kappa_rim[1:-1, :-2, 1:-1]),
        0.5 * (centre + kappa_rim[1:-1, 1:-1, 2:]),
        0.5 * (centre + kappa_rim[1:-1, 1:-1, :-2]),
    )


def solid_operator(bordered_grid_data, faces, diagonal):
    centre = bordered_grid_data[1:-1, 1:-1, 1:-1]
    flows = (
        faces[0] * bordered_grid_data[2:, 1:-1, 1:-1]
        + faces[1] * bordered_grid_data[:-2, 1:-1, 1:-1]
    )
    flows = (
        flows
        + faces[2] * bordered_grid_data[1:-1, 2:, 1:-1]
        + faces[3] * bordered_grid_data[1:-1, :-2, 1:-1]
    )
    flows = (
        flows
        + faces[4] * bordered_grid_data[1:-1, 1:-1, 2:]
        + faces[5] * bordered_grid_data[1:-1, 1:-1, :-2]
    )
    return diagonal * centre - flows


def pad_depth(array):
    widths = [(0, 0)] * (array.ndim - 1) + [(1, 1)]
    return jnp.pad(array, widths)


def shards(
    fluid_adjoint_in,
    fluid_source,
    velocity,
    diffusion,
    jacobian,
    wall_coefficient,
    metal_costate_prior,
    solid_source,
    conductivity,
    tile_owner,
    tile_target,
):
    highest = lax.Precision.HIGHEST
    spread = diffusion[:, None, None, None]
    fluid_diagonal = (
        6.0 * spread
        + (velocity[0] + velocity[1] + velocity[2])
        + jnp.diagonal(jacobian)[:, None, None, None]
    )
    adjoint = fluid_adjoint_in
    for iteration in range(FSWEEPS):
        bordered_grid_data = padded(adjoint, (("blk", 1), ("span", 2)), 1)
        bordered_grid_data = pad_depth(bordered_grid_data)
        fluid_residual = fluid_source - fluid_operator(
            bordered_grid_data, velocity, spread, jacobian
        )
        adjoint = adjoint + damping_weight * fluid_residual / fluid_diagonal
    fluid_squares = jnp.sum(fluid_residual * fluid_residual, axis=(1, 2, 3))
    wall_flux = wall_coefficient[0] * adjoint[4, 0]
    rows = wall_flux.shape[0]
    blocks = lax.axis_size("blk")
    myself = lax.axis_index("blk")
    owner_local = tile_owner[0, :, 0]
    target_local = tile_target[0, :]
    owners_all, targets_all = (
        lax.all_gather(owner_local, "blk", axis=0, tiled=True),
        lax.all_gather(target_local, "blk", axis=0, tiled=True),
    )
    owner_grid = owners_all.reshape(blocks, rows)
    target_grid = targets_all.reshape(blocks, rows)
    to_myself = owner_grid == myself
    target_hot = target_grid[:, :, None] == jnp.arange(rows, dtype=jnp.int32)[None, None, :]
    placing = (target_hot & to_myself[:, :, None]).astype(jnp.float32).reshape(blocks * rows, rows)
    arrived = lax.all_gather(wall_flux, "blk", axis=0, tiled=True)
    surface = jnp.dot(placing.T, arrived, precision=highest)
    heat_source = solid_source.at[-1].add(surface)
    thermal_state_grid = metal_costate_prior
    kappa_rim = padded(conductivity, (("blk", 0), ("span", 1)), 1)
    kappa_rim = pad_depth(kappa_rim)
    faces = face_conductance(kappa_rim)
    metal_pivot_entries = faces[0] + faces[1] + faces[2] + faces[3] + faces[4] + faces[5]
    for iteration in range(SSWEEPS):
        bordered_grid_data = padded(thermal_state_grid, (("blk", 0), ("span", 1)), 1)
        bordered_grid_data = pad_depth(bordered_grid_data)
        metal_imbalance_grid = heat_source - solid_operator(
            bordered_grid_data, faces, metal_pivot_entries
        )
        thermal_state_grid = (
            thermal_state_grid + damping_weight * metal_imbalance_grid / metal_pivot_entries
        )
    interface_heat_level = thermal_state_grid[-1]
    boundary_patches_finished = lax.all_gather(interface_heat_level, "blk", axis=0, tiled=True)
    output_entries = jnp.take(boundary_patches_finished, owner_local * rows + target_local, axis=0)
    gas_outcome = adjoint.at[4, 0].add(wall_coefficient[0] * output_entries)
    solid_squares = jnp.sum(metal_imbalance_grid * metal_imbalance_grid)[None]
    totals = lax.psum(jnp.concatenate([fluid_squares, solid_squares]), ("blk", "span"))
    every_processor = lax.axis_size("blk") * lax.axis_size("span")
    fluid_cells = float(adjoint.shape[1] * adjoint.shape[2] * adjoint.shape[3] * every_processor)
    solid_cells = float(
        thermal_state_grid.shape[0]
        * thermal_state_grid.shape[1]
        * thermal_state_grid.shape[2]
        * every_processor
    )
    counts = jnp.array([fluid_cells] * 5 + [solid_cells], jnp.float32)
    magnitude_list = jnp.sqrt(totals / counts)
    return (gas_outcome, thermal_state_grid, magnitude_list)


def solution(mesh):
    placed = (
        P(None, "blk", "span", None),
        P(None, "blk", "span", None),
        P(None, "blk", "span", None),
        P(),
        P(),
        P("blk", "span", None),
        P("blk", "span", None),
        P("blk", "span", None),
        P("blk", "span", None),
        P("span", "blk", None),
        P("span", "blk"),
    )
    return jax.shard_map(
        shards,
        mesh=mesh,
        in_specs=placed,
        out_specs=(P(None, "blk", "span", None), P("blk", "span", None), P()),
        check_vma=False,
    )
```

profile of v0, /device:TPU:2, one launch (start us, length us, event | category | flops | bytes accessed | tf_op | source)
XLA Modules:
  0.0 370.5 jit_solution(5415000750408817278)
XLA Ops:
  3.0 3.4 collective-permute-start.1
  9.6 3.4 collective-permute-start.17
  15.5 3.4 collective-permute-start.21
  20.5 26.2 %all-reduce.11 = (s32[1024]{0:T(1024)S(1)}, s32[1024]{0:T(1024)S(1)}) all-reduce(s32[1024]{0:T(1024)S(1)} %bitcast_dynamic-update-slice_fusion.1, s32[1024]{0:T(1024)S(1)} %bitcast_dynamic-update-slice_fusion), channel_id=2, replica_groups=mesh['blk'=32,'span'=8] {'blk'}, use_global_device_ids=true, to_apply=%add.9 | all-reduce | flops 2048 | bytes 16384
  47.4 2.5 collective-permute-start.20
  51.8 3.0 collective-permute-start.3
  56.2 3.7 %collective-permute-start.19 = (f32[18,1,128]{2,1,0:T(1,128)S(1)}, f32[18,1,128]{2,1,0:T(1,128)S(1)}, u32[]{:S(2)}, u32[]{:S(2)}) collective-permute-start(f32[18,1,128]{2,1,0:T(1,128)S(1)} %get-tuple-element.70), channel_id=1, source_target_pairs={{0,1},{1,2},{2,3},{3,4},{4,5},{5,6},{6,7},{8,9},{9,10},{10,11},{11... | collective-permute-start | bytes 27656 | tf_op jit(solution)/shard_map/ppermute | solution.py:16
  60.7 2.7 fusion.10
  65.4 3.9 %collective-permute-start.5 = (f32[5,1,32,128]{3,0,2,1:T(8,128)S(1)}, f32[5,1,32,128]{3,0,2,1:T(8,128)S(1)}, u32[]{:S(2)}, u32[]{:S(2)}) collective-permute-start(f32[5,1,32,128]{3,0,2,1:T(8,128)S(1)} %get-tuple-element.56), channel_id=1, source_target_pairs={{0,8},{8,16},{16,24},{24,32},{32,40},{40,48},{48,56},{56,64},{64,7... | collective-permute-start | bytes 245768 | tf_op jit(solution)/shard_map/ppermute | solution.py:16
  74.2 3.1 collective-permute-start.7
  83.1 4.2 %collective-permute-start.9 = (f32[5,1,32,128]{3,0,2,1:T(8,128)S(1)}, f32[5,1,32,128]{3,0,2,1:T(8,128)S(1)}, u32[]{:S(2)}, u32[]{:S(2)}) collective-permute-start(f32[5,1,32,128]{3,0,2,1:T(8,128)S(1)} %get-tuple-element.54), channel_id=1, source_target_pairs={{0,8},{8,16},{16,24},{24,32},{32,40},{40,48},{48,56},{56,64},{64,7... | collective-permute-start | bytes 245768 | tf_op jit(solution)/shard_map/ppermute | solution.py:16
  91.8 3.3 collective-permute-start.11
  96.5 5.7 %collective-permute-start.23 = (f32[18,1,128]{2,1,0:T(1,128)S(1)}, f32[18,1,128]{2,1,0:T(1,128)S(1)}, u32[]{:S(2)}, u32[]{:S(2)}) collective-permute-start(f32[18,1,128]{2,1,0:T(1,128)S(1)} %get-tuple-element.72), channel_id=1, source_target_pairs={{0,1},{1,2},{2,3},{3,4},{4,5},{5,6},{6,7},{8,9},{9,10},{10,11},{11... | collective-permute-start | bytes 27656 | tf_op jit(solution)/shard_map/ppermute | solution.py:16
  107.2 3.9 %collective-permute-start.13 = (f32[5,1,32,128]{3,0,2,1:T(8,128)S(1)}, f32[5,1,32,128]{3,0,2,1:T(8,128)S(1)}, u32[]{:S(2)}, u32[]{:S(2)}) collective-permute-start(f32[5,1,32,128]{3,0,2,1:T(8,128)S(1)} %get-tuple-element.52), channel_id=1, source_target_pairs={{0,8},{8,16},{16,24},{24,32},{32,40},{40,48},{48,56},{56,64},{64,7... | collective-permute-start | bytes 245768 | tf_op jit(solution)/shard_map/ppermute | solution.py:16
  116.2 3.1 collective-permute-start.15
  123.5 59.1 %all_gather.14 = f32[1024,128]{1,0:T(8,128)S(1)} all-gather(f32[32,128]{1,0:T(8,128)S(1)} %bitcast_multiply_fusion), channel_id=1, replica_groups=mesh['blk'=32,'span'=8] {'blk'}, dimensions={0}, use_global_device_ids=true | all-gather | bytes 540672 | tf_op jit(solution)/shard_map/all_gather | solution.py:129
  186.0 3.9 %collective-permute-start.25 = (f32[1,32,128]{2,1,0:T(8,128)S(1)}, f32[1,32,128]{2,1,0:T(8,128)S(1)}, u32[]{:S(2)}, u32[]{:S(2)}) collective-permute-start(f32[1,32,128]{2,1,0:T(8,128)S(1)} %get-tuple-element.78), channel_id=1, source_target_pairs={{0,8},{8,16},{16,24},{24,32},{32,40},{40,48},{48,56},{56,64},{64,7... | collective-permute-start | bytes 49160 | tf_op jit(solution)/shard_map/ppermute | solution.py:16
  192.9 3.0 collective-permute-start.27
  199.4 3.9 %collective-permute-start.29 = (f32[1,32,128]{2,1,0:T(8,128)S(1)}, f32[1,32,128]{2,1,0:T(8,128)S(1)}, u32[]{:S(2)}, u32[]{:S(2)}) collective-permute-start(f32[1,32,128]{2,1,0:T(8,128)S(1)} %get-tuple-element.76), channel_id=1, source_target_pairs={{0,8},{8,16},{16,24},{24,32},{32,40},{40,48},{48,56},{56,64},{64,7... | collective-permute-start | bytes 49160 | tf_op jit(solution)/shard_map/ppermute | solution.py:16
  206.4 5.1 %collective-permute-start.31 = (f32[18,1,128]{2,1,0:T(1,128)S(1)}, f32[18,1,128]{2,1,0:T(1,128)S(1)}, u32[]{:S(2)}, u32[]{:S(2)}) collective-permute-start(f32[18,1,128]{2,1,0:T(1,128)S(1)} %get-tuple-element.66), channel_id=1, source_target_pairs={{0,1},{1,2},{2,3},{3,4},{4,5},{5,6},{6,7},{8,9},{9,10},{10,11},{11... | collective-permute-start | bytes 27656 | tf_op jit(solution)/shard_map/ppermute | solution.py:16
  215.0 4.2 %collective-permute-start.33 = (f32[1,32,128]{2,1,0:T(8,128)S(1)}, f32[1,32,128]{2,1,0:T(8,128)S(1)}, u32[]{:S(2)}, u32[]{:S(2)}) collective-permute-start(f32[1,32,128]{2,1,0:T(8,128)S(1)} %get-tuple-element.74), channel_id=1, source_target_pairs={{0,8},{8,16},{16,24},{24,32},{32,40},{40,48},{48,56},{56,64},{64,7... | collective-permute-start | bytes 49160 | tf_op jit(solution)/shard_map/ppermute | solution.py:16
  222.0 4.8 %collective-permute-start.35 = (f32[18,1,128]{2,1,0:T(1,128)S(1)}, f32[18,1,128]{2,1,0:T(1,128)S(1)}, u32[]{:S(2)}, u32[]{:S(2)}) collective-permute-start(f32[18,1,128]{2,1,0:T(1,128)S(1)} %get-tuple-element.64), channel_id=1, source_target_pairs={{0,1},{1,2},{2,3},{3,4},{4,5},{5,6},{6,7},{8,9},{9,10},{10,11},{11... | collective-permute-start | bytes 27656 | tf_op jit(solution)/shard_map/ppermute | solution.py:16
  229.6 89.1 %psum.7 = f32[6]{0:T(128)S(1)} all-reduce(f32[6]{0:T(128)S(1)} %pad_maximum_fusion.78), channel_id=1, replica_groups=mesh['blk'=32,'span'=8] {'blk','span'}, use_global_device_ids=true, to_apply=%region_2.3 | all-reduce | flops 6 | bytes 48 | tf_op jit(solution)/shard_map/psum | solution.py:151
  318.9 49.3 %all-gather.2 = f32[1,1024,128]{2,1,0:T(8,128)S(1)} all-gather(f32[1,32,128]{2,1,0:T(8,128)S(1)} %slice.616), channel_id=4, replica_groups=mesh['blk'=32,'span'=8] {'blk'}, dimensions={1}, use_global_device_ids=true | all-gather | bytes 540672 | tf_op jit(solution)/shard_map/all_gather | solution.py:147
  (161 shorter events, 70.1 us)
Async XLA Ops:
  3.0 46.9 %collective-permute-start.1 = (f32[5,1,32,128]{3,0,2,1:T(8,128)}, f32[5,1,32,128]{3,0,2,1:T(8,128)S(1)}, u32[]{:S(2)}, u32[]{:S(2)}) collective-permute-start(f32[5,1,32,128]{3,0,2,1:T(8,128)} %get-tuple-element.59), channel_id=1, source_target_pairs={{0,8},{8,16},{16,24},{24,32},{32,40},{40,48},{48,56},{56,64},{64,7... | collective-permute-start | bytes 245768 | tf_op jit(solution)/shard_map/ppermute | solution.py:16
  6.4 44.0 %collective-permute-start = (f32[5,1,32,128]{3,0,2,1:T(8,128)}, f32[5,1,32,128]{3,0,2,1:T(8,128)S(1)}, u32[]{:S(2)}, u32[]{:S(2)}) collective-permute-start(f32[5,1,32,128]{3,0,2,1:T(8,128)} %get-tuple-element.58), channel_id=1, source_target_pairs={{8,0},{16,8},{24,16},{32,24},{40,32},{48,40},{56,48},{64,56},{72,6... | collective-permute-start | bytes 245768 | tf_op jit(solution)/shard_map/ppermute | solution.py:19
  9.6 37.7 %collective-permute-start.17 = (f32[1,32,128]{2,1,0:T(8,128)S(1)}, f32[1,32,128]{2,1,0:T(8,128)S(1)}, u32[]{:S(2)}, u32[]{:S(2)}) collective-permute-start(f32[1,32,128]{2,1,0:T(8,128)S(1)} %get-tuple-element.80), channel_id=1, source_target_pairs={{0,8},{8,16},{16,24},{24,32},{32,40},{40,48},{48,56},{56,64},{64,7... | collective-permute-start | bytes 49160 | tf_op jit(solution)/shard_map/ppermute | solution.py:16
  13.0 36.9 %collective-permute-start.16 = (f32[1,32,128]{2,1,0:T(8,128)S(1)}, f32[1,32,128]{2,1,0:T(8,128)S(1)}, u32[]{:S(2)}, u32[]{:S(2)}) collective-permute-start(f32[1,32,128]{2,1,0:T(8,128)S(1)} %get-tuple-element.81), channel_id=1, source_target_pairs={{8,0},{16,8},{24,16},{32,24},{40,32},{48,40},{56,48},{64,56},{72,6... | collective-permute-start | bytes 49160 | tf_op jit(solution)/shard_map/ppermute | solution.py:19
  15.5 49.9 %collective-permute-start.21 = (f32[1,32,128]{2,1,0:T(8,128)S(1)}, f32[1,32,128]{2,1,0:T(8,128)S(1)}, u32[]{:S(2)}, u32[]{:S(2)}) collective-permute-start(f32[1,32,128]{2,1,0:T(8,128)S(1)} %get-tuple-element.83), channel_id=1, source_target_pairs={{0,8},{8,16},{16,24},{24,32},{32,40},{40,48},{48,56},{56,64},{64,7... | collective-permute-start | bytes 49160 | tf_op jit(solution)/shard_map/ppermute | solution.py:16
  47.4 39.9 %collective-permute-start.20 = (f32[1,32,128]{2,1,0:T(8,128)S(1)}, f32[1,32,128]{2,1,0:T(8,128)S(1)}, u32[]{:S(2)}, u32[]{:S(2)}) collective-permute-start(f32[1,32,128]{2,1,0:T(8,128)S(1)} %get-tuple-element.82), channel_id=1, source_target_pairs={{8,0},{16,8},{24,16},{32,24},{40,32},{48,40},{56,48},{64,56},{72,6... | collective-permute-start | bytes 49160 | tf_op jit(solution)/shard_map/ppermute | solution.py:19
  51.8 8.1 %collective-permute-start.3 = (f32[5,10,1,128]{3,0,2,1:T(8,128)S(1)}, f32[5,10,1,128]{3,0,2,1:T(8,128)S(1)}, u32[]{:S(2)}, u32[]{:S(2)}) collective-permute-start(f32[5,10,1,128]{3,0,2,1:T(8,128)S(1)} %get-tuple-element.48), channel_id=1, source_target_pairs={{0,1},{1,2},{2,3},{3,4},{4,5},{5,6},{6,7},{8,9},{9,10},{10,11},{11... | collective-permute-start | bytes 76808 | tf_op jit(solution)/shard_map/ppermute | solution.py:16
  54.8 52.3 %collective-permute-start.18 = (f32[18,1,128]{2,1,0:T(1,128)S(1)}, f32[18,1,128]{2,1,0:T(1,128)S(1)}, u32[]{:S(2)}, u32[]{:S(2)}) collective-permute-start(f32[18,1,128]{2,1,0:T(1,128)S(1)} %get-tuple-element.71), channel_id=1, source_target_pairs={{1,0},{2,1},{3,2},{4,3},{5,4},{6,5},{7,6},{9,8},{10,9},{11,10},{12... | collective-permute-start | bytes 27656 | tf_op jit(solution)/shard_map/ppermute | solution.py:19
  56.2 54.9 %collective-permute-start.19 = (f32[18,1,128]{2,1,0:T(1,128)S(1)}, f32[18,1,128]{2,1,0:T(1,128)S(1)}, u32[]{:S(2)}, u32[]{:S(2)}) collective-permute-start(f32[18,1,128]{2,1,0:T(1,128)S(1)} %get-tuple-element.70), channel_id=1, source_target_pairs={{0,1},{1,2},{2,3},{3,4},{4,5},{5,6},{6,7},{8,9},{9,10},{10,11},{11... | collective-permute-start | bytes 27656 | tf_op jit(solution)/shard_map/ppermute | solution.py:16
  63.4 7.5 %collective-permute-start.4 = (f32[5,1,32,128]{3,0,2,1:T(8,128)S(1)}, f32[5,1,32,128]{3,0,2,1:T(8,128)S(1)}, u32[]{:S(2)}, u32[]{:S(2)}) collective-permute-start(f32[5,1,32,128]{3,0,2,1:T(8,128)S(1)} %get-tuple-element.57), channel_id=1, source_target_pairs={{8,0},{16,8},{24,16},{32,24},{40,32},{48,40},{56,48},{64,56},{72,6... | collective-permute-start | bytes 245768 | tf_op jit(solution)/shard_map/ppermute | solution.py:19
  65.4 7.5 %collective-permute-start.5 = (f32[5,1,32,128]{3,0,2,1:T(8,128)S(1)}, f32[5,1,32,128]{3,0,2,1:T(8,128)S(1)}, u32[]{:S(2)}, u32[]{:S(2)}) collective-permute-start(f32[5,1,32,128]{3,0,2,1:T(8,128)S(1)} %get-tuple-element.56), channel_id=1, source_target_pairs={{0,8},{8,16},{16,24},{24,32},{32,40},{40,48},{48,56},{56,64},{64,7... | collective-permute-start | bytes 245768 | tf_op jit(solution)/shard_map/ppermute | solution.py:16
  81.2 7.5 %collective-permute-start.8 = (f32[5,1,32,128]{3,0,2,1:T(8,128)S(1)}, f32[5,1,32,128]{3,0,2,1:T(8,128)S(1)}, u32[]{:S(2)}, u32[]{:S(2)}) collective-permute-start(f32[5,1,32,128]{3,0,2,1:T(8,128)S(1)} %get-tuple-element.55), channel_id=1, source_target_pairs={{8,0},{16,8},{24,16},{32,24},{40,32},{48,40},{56,48},{64,56},{72,6... | collective-permute-start | bytes 245768 | tf_op jit(solution)/shard_map/ppermute | solution.py:19
  83.1 7.4 %collective-permute-start.9 = (f32[5,1,32,128]{3,0,2,1:T(8,128)S(1)}, f32[5,1,32,128]{3,0,2,1:T(8,128)S(1)}, u32[]{:S(2)}, u32[]{:S(2)}) collective-permute-start(f32[5,1,32,128]{3,0,2,1:T(8,128)S(1)} %get-tuple-element.54), channel_id=1, source_target_pairs={{0,8},{8,16},{16,24},{24,32},{32,40},{40,48},{48,56},{56,64},{64,7... | collective-permute-start | bytes 245768 | tf_op jit(solution)/shard_map/ppermute | solution.py:16
  90.5 6.0 %collective-permute-start.10 = (f32[5,10,1,128]{3,0,2,1:T(8,128)S(1)}, f32[5,10,1,128]{3,0,2,1:T(8,128)S(1)}, u32[]{:S(2)}, u32[]{:S(2)}) collective-permute-start(f32[5,10,1,128]{3,0,2,1:T(8,128)S(1)} %get-tuple-element.45), channel_id=1, source_target_pairs={{1,0},{2,1},{3,2},{4,3},{5,4},{6,5},{7,6},{9,8},{10,9},{11,10},{12... | collective-permute-start | bytes 76808 | tf_op jit(solution)/shard_map/ppermute | solution.py:19
  91.8 10.4 %collective-permute-start.11 = (f32[5,10,1,128]{3,0,2,1:T(8,128)S(1)}, f32[5,10,1,128]{3,0,2,1:T(8,128)S(1)}, u32[]{:S(2)}, u32[]{:S(2)}) collective-permute-start(f32[5,10,1,128]{3,0,2,1:T(8,128)S(1)} %get-tuple-element.44), channel_id=1, source_target_pairs={{0,1},{1,2},{2,3},{3,4},{4,5},{5,6},{6,7},{8,9},{9,10},{10,11},{11... | collective-permute-start | bytes 76808 | tf_op jit(solution)/shard_map/ppermute | solution.py:16
  95.2 24.1 %collective-permute-start.22 = (f32[18,1,128]{2,1,0:T(1,128)S(1)}, f32[18,1,128]{2,1,0:T(1,128)S(1)}, u32[]{:S(2)}, u32[]{:S(2)}) collective-permute-start(f32[18,1,128]{2,1,0:T(1,128)S(1)} %get-tuple-element.73), channel_id=1, source_target_pairs={{1,0},{2,1},{3,2},{4,3},{5,4},{6,5},{7,6},{9,8},{10,9},{11,10},{12... | collective-permute-start | bytes 27656 | tf_op jit(solution)/shard_map/ppermute | solution.py:19
  96.5 22.8 %collective-permute-start.23 = (f32[18,1,128]{2,1,0:T(1,128)S(1)}, f32[18,1,128]{2,1,0:T(1,128)S(1)}, u32[]{:S(2)}, u32[]{:S(2)}) collective-permute-start(f32[18,1,128]{2,1,0:T(1,128)S(1)} %get-tuple-element.72), channel_id=1, source_target_pairs={{0,1},{1,2},{2,3},{3,4},{4,5},{5,6},{6,7},{8,9},{9,10},{10,11},{11... | collective-permute-start | bytes 27656 | tf_op jit(solution)/shard_map/ppermute | solution.py:16
  105.2 7.2 %collective-permute-start.12 = (f32[5,1,32,128]{3,0,2,1:T(8,128)S(1)}, f32[5,1,32,128]{3,0,2,1:T(8,128)S(1)}, u32[]{:S(2)}, u32[]{:S(2)}) collective-permute-start(f32[5,1,32,128]{3,0,2,1:T(8,128)S(1)} %get-tuple-element.53), channel_id=1, source_target_pairs={{8,0},{16,8},{24,16},{32,24},{40,32},{48,40},{56,48},{64,56},{72,6... | collective-permute-start | bytes 245768 | tf_op jit(solution)/shard_map/ppermute | solution.py:19
  107.2 7.5 %collective-permute-start.13 = (f32[5,1,32,128]{3,0,2,1:T(8,128)S(1)}, f32[5,1,32,128]{3,0,2,1:T(8,128)S(1)}, u32[]{:S(2)}, u32[]{:S(2)}) collective-permute-start(f32[5,1,32,128]{3,0,2,1:T(8,128)S(1)} %get-tuple-element.52), channel_id=1, source_target_pairs={{0,8},{8,16},{16,24},{24,32},{32,40},{40,48},{48,56},{56,64},{64,7... | collective-permute-start | bytes 245768 | tf_op jit(solution)/shard_map/ppermute | solution.py:16
  184.0 5.9 %collective-permute-start.24 = (f32[1,32,128]{2,1,0:T(8,128)S(1)}, f32[1,32,128]{2,1,0:T(8,128)S(1)}, u32[]{:S(2)}, u32[]{:S(2)}) collective-permute-start(f32[1,32,128]{2,1,0:T(8,128)S(1)} %get-tuple-element.79), channel_id=1, source_target_pairs={{8,0},{16,8},{24,16},{32,24},{40,32},{48,40},{56,48},{64,56},{72,6... | collective-permute-start | bytes 49160 | tf_op jit(solution)/shard_map/ppermute | solution.py:19
  205.1 6.4 %collective-permute-start.30 = (f32[18,1,128]{2,1,0:T(1,128)S(1)}, f32[18,1,128]{2,1,0:T(1,128)S(1)}, u32[]{:S(2)}, u32[]{:S(2)}) collective-permute-start(f32[18,1,128]{2,1,0:T(1,128)S(1)} %get-tuple-element.67), channel_id=1, source_target_pairs={{1,0},{2,1},{3,2},{4,3},{5,4},{6,5},{7,6},{9,8},{10,9},{11,10},{12... | collective-permute-start | bytes 27656 | tf_op jit(solution)/shard_map/ppermute | solution.py:19
  206.4 5.9 %collective-permute-start.31 = (f32[18,1,128]{2,1,0:T(1,128)S(1)}, f32[18,1,128]{2,1,0:T(1,128)S(1)}, u32[]{:S(2)}, u32[]{:S(2)}) collective-permute-start(f32[18,1,128]{2,1,0:T(1,128)S(1)} %get-tuple-element.66), channel_id=1, source_target_pairs={{0,1},{1,2},{2,3},{3,4},{4,5},{5,6},{6,7},{8,9},{9,10},{10,11},{11... | collective-permute-start | bytes 27656 | tf_op jit(solution)/shard_map/ppermute | solution.py:16
  213.1 6.2 %collective-permute-start.32 = (f32[1,32,128]{2,1,0:T(8,128)S(1)}, f32[1,32,128]{2,1,0:T(8,128)S(1)}, u32[]{:S(2)}, u32[]{:S(2)}) collective-permute-start(f32[1,32,128]{2,1,0:T(8,128)S(1)} %get-tuple-element.75), channel_id=1, source_target_pairs={{8,0},{16,8},{24,16},{32,24},{40,32},{48,40},{56,48},{64,56},{72,6... | collective-permute-start | bytes 49160 | tf_op jit(solution)/shard_map/ppermute | solution.py:19
  220.7 6.1 %collective-permute-start.34 = (f32[18,1,128]{2,1,0:T(1,128)S(1)}, f32[18,1,128]{2,1,0:T(1,128)S(1)}, u32[]{:S(2)}, u32[]{:S(2)}) collective-permute-start(f32[18,1,128]{2,1,0:T(1,128)S(1)} %get-tuple-element.65), channel_id=1, source_target_pairs={{1,0},{2,1},{3,2},{4,3},{5,4},{6,5},{7,6},{9,8},{10,9},{11,10},{12... | collective-permute-start | bytes 27656 | tf_op jit(solution)/shard_map/ppermute | solution.py:19
  (32 other events, 851.3 us)
where the time goes:
time: 372 us; the launch traced here: 370 us
  blocking collectives  224 us (60%)
  starting transfers between devices  99.9 us (27%)
  waiting for transfers between devices  18.5 us (5%)
  matrix products  10.4 us (3%)
  other arithmetic  8.88 us (2%)
  local copies, waits for them, and re-layouts  6.83 us (2%)
    psum x1, blocking collectives, shards(): lax.psum(jnp.concatenate([fluid_squares, solid_squares]), ('blk', 'span'))  89.1 us
    ppermute x18, starting transfers between devices, padded(): lax.ppermute(lax.slice_in_dim(block, block.shape[dim] - width, None, axis...  69.2 us
    all_gather x1, blocking collectives, shards(): arrived = lax.all_gather(wall_flux, 'blk', axis=0, tiled=True)  59.1 us
    all_gather x1, blocking collectives, shards(): lax.all_gather(interface_heat_level, 'blk', axis=0, tiled=True)  49.3 us
    ppermute x18, starting transfers between devices, padded(): lax.ppermute(lax.slice_in_dim(block, 0, width, axis=dim), axis, backward)  30.7 us
    unnamed x1, blocking collectives  26.2 us
    ppermute x18, waiting for transfers between devices, padded(): lax.ppermute(lax.slice_in_dim(block, block.shape[dim] - width, None, axis...  14.4 us
    dot_general x4, matrix products, fluid_operator(): jnp.einsum('fg,gxyz->fxyz', jacobian, centre, precision=lax.Precision.HIG...  9.52 us
  transfers between devices with their start and end apart: 36, of which 14 were waited for; matrix products, arithmetic and copies ran while one was open for 4% of the time, Pallas kernels for 0%

commit v1 on v0

--- a/solution.py
+++ b/solution.py
@@ -148,7 +148,13 @@
     output_entries = jnp.take(boundary_patches_finished, owner_local * rows + target_local, axis=0)
     gas_outcome = adjoint.at[4, 0].add(wall_coefficient[0] * output_entries)
     solid_squares = jnp.sum(metal_imbalance_grid * metal_imbalance_grid)[None]
-    totals = lax.psum(jnp.concatenate([fluid_squares, solid_squares]), ("blk", "span"))
+
+    def assign_halves_for(arr):
+        for nth in ("blk", "span"):
+            arr = lax.psum(arr, nth)
+        return arr
+
+    totals = assign_halves_for(jnp.concatenate([fluid_squares, solid_squares]))
     every_processor = lax.axis_size("blk") * lax.axis_size("span")
     fluid_cells = float(adjoint.shape[1] * adjoint.shape[2] * adjoint.shape[3] * every_processor)
     solid_cells = float(

time: 372 us -> 380 us (1.022)
  blocking collectives: 224 us -> 230 us
    psum x1 -> x2, blocking collectives: 89.1 us -> 92.9 us  [assign_halves_for(): arr = lax.psum(arr, nth)]
  transfers between devices with their start and end apart: 36 -> 36, of which waited for: 14 -> 14; matrix products, arithmetic and copies ran while one was open for 4% -> 3% of each run, Pallas kernels for 0% -> 0%
where the time goes in v1:
time: 380 us; the launch traced here: 377 us
  blocking collectives  230 us (61%)
  starting transfers between devices  99.9 us (26%)
  waiting for transfers between devices  18.5 us (5%)
  matrix products  10.4 us (3%)
  other arithmetic  8.88 us (2%)
  local copies, waits for them, and re-layouts  6.84 us (2%)
    psum x2, blocking collectives, assign_halves_for(): arr = lax.psum(arr, nth)  92.9 us
    ppermute x18, starting transfers between devices, padded(): lax.ppermute(lax.slice_in_dim(block, block.shape[dim] - width, None, axis...  69.2 us
    all_gather x1, blocking collectives, shards(): arrived = lax.all_gather(wall_flux, 'blk', axis=0, tiled=True)  59.1 us
    all_gather x1, blocking collectives, shards(): lax.all_gather(interface_heat_level, 'blk', axis=0, tiled=True)  52.2 us
    ppermute x18, starting transfers between devices, padded(): lax.ppermute(lax.slice_in_dim(block, 0, width, axis=dim), axis, backward)  30.7 us
    unnamed x1, blocking collectives  26.2 us
    ppermute x18, waiting for transfers between devices, padded(): lax.ppermute(lax.slice_in_dim(block, block.shape[dim] - width, None, axis...  14.5 us
    dot_general x4, matrix products, fluid_operator(): jnp.einsum('fg,gxyz->fxyz', jacobian, centre, precision=lax.Precision.HIG...  9.52 us
  transfers between devices with their start and end apart: 36, of which 14 were waited for; matrix products, arithmetic and copies ran while one was open for 3% of the time, Pallas kernels for 0%

profile of v1, /device:TPU:2, one launch (start us, length us, event | category | flops | bytes accessed | tf_op | source)
XLA Modules:
  0.0 377.2 jit_solution(12776028832704254321)
XLA Ops:
  3.0 3.4 collective-permute-start.1
  9.6 3.4 collective-permute-start.17
  15.5 3.4 collective-permute-start.21
  20.5 26.2 %all-reduce.11 = (s32[1024]{0:T(1024)S(1)}, s32[1024]{0:T(1024)S(1)}) all-reduce(s32[1024]{0:T(1024)S(1)} %bitcast_dynamic-update-slice_fusion.1, s32[1024]{0:T(1024)S(1)} %bitcast_dynamic-update-slice_fusion), channel_id=2, replica_groups=mesh['blk'=32,'span'=8] {'blk'}, use_global_device_ids=true, to_apply=%add.9 | all-reduce | flops 2048 | bytes 16384
  51.8 3.0 collective-permute-start.3
  56.2 3.7 collective-permute-start.19
  60.7 2.7 fusion.10
  65.4 3.9 %collective-permute-start.5 = (f32[5,1,32,128]{3,0,2,1:T(8,128)S(1)}, f32[5,1,32,128]{3,0,2,1:T(8,128)S(1)}, u32[]{:S(2)}, u32[]{:S(2)}) collective-permute-start(f32[5,1,32,128]{3,0,2,1:T(8,128)S(1)} %get-tuple-element.56), channel_id=1, source_target_pairs={{0,8},{8,16},{16,24},{24,32},{32,40},{40,48},{48,56},{56,64},{64,7... | collective-permute-start | bytes 245768 | tf_op jit(solution)/shard_map/ppermute | solution.py:16
  74.2 3.1 collective-permute-start.7
  83.1 4.2 %collective-permute-start.9 = (f32[5,1,32,128]{3,0,2,1:T(8,128)S(1)}, f32[5,1,32,128]{3,0,2,1:T(8,128)S(1)}, u32[]{:S(2)}, u32[]{:S(2)}) collective-permute-start(f32[5,1,32,128]{3,0,2,1:T(8,128)S(1)} %get-tuple-element.54), channel_id=1, source_target_pairs={{0,8},{8,16},{16,24},{24,32},{32,40},{40,48},{48,56},{56,64},{64,7... | collective-permute-start | bytes 245768 | tf_op jit(solution)/shard_map/ppermute | solution.py:16
  91.8 3.4 collective-permute-start.11
  96.5 5.7 %collective-permute-start.23 = (f32[18,1,128]{2,1,0:T(1,128)S(1)}, f32[18,1,128]{2,1,0:T(1,128)S(1)}, u32[]{:S(2)}, u32[]{:S(2)}) collective-permute-start(f32[18,1,128]{2,1,0:T(1,128)S(1)} %get-tuple-element.72), channel_id=1, source_target_pairs={{0,1},{1,2},{2,3},{3,4},{4,5},{5,6},{6,7},{8,9},{9,10},{10,11},{11... | collective-permute-start | bytes 27656 | tf_op jit(solution)/shard_map/ppermute | solution.py:16
  107.2 3.9 %collective-permute-start.13 = (f32[5,1,32,128]{3,0,2,1:T(8,128)S(1)}, f32[5,1,32,128]{3,0,2,1:T(8,128)S(1)}, u32[]{:S(2)}, u32[]{:S(2)}) collective-permute-start(f32[5,1,32,128]{3,0,2,1:T(8,128)S(1)} %get-tuple-element.52), channel_id=1, source_target_pairs={{0,8},{8,16},{16,24},{24,32},{32,40},{40,48},{48,56},{56,64},{64,7... | collective-permute-start | bytes 245768 | tf_op jit(solution)/shard_map/ppermute | solution.py:16
  116.2 3.1 collective-permute-start.15
  123.5 59.1 %all_gather.14 = f32[1024,128]{1,0:T(8,128)S(1)} all-gather(f32[32,128]{1,0:T(8,128)S(1)} %bitcast_multiply_fusion), channel_id=1, replica_groups=mesh['blk'=32,'span'=8] {'blk'}, dimensions={0}, use_global_device_ids=true | all-gather | bytes 540672 | tf_op jit(solution)/shard_map/all_gather | solution.py:129
  186.0 3.9 %collective-permute-start.25 = (f32[1,32,128]{2,1,0:T(8,128)S(1)}, f32[1,32,128]{2,1,0:T(8,128)S(1)}, u32[]{:S(2)}, u32[]{:S(2)}) collective-permute-start(f32[1,32,128]{2,1,0:T(8,128)S(1)} %get-tuple-element.78), channel_id=1, source_target_pairs={{0,8},{8,16},{16,24},{24,32},{32,40},{40,48},{48,56},{56,64},{64,7... | collective-permute-start | bytes 49160 | tf_op jit(solution)/shard_map/ppermute | solution.py:16
  193.0 3.0 collective-permute-start.27
  199.5 3.9 %collective-permute-start.29 = (f32[1,32,128]{2,1,0:T(8,128)S(1)}, f32[1,32,128]{2,1,0:T(8,128)S(1)}, u32[]{:S(2)}, u32[]{:S(2)}) collective-permute-start(f32[1,32,128]{2,1,0:T(8,128)S(1)} %get-tuple-element.76), channel_id=1, source_target_pairs={{0,8},{8,16},{16,24},{24,32},{32,40},{40,48},{48,56},{56,64},{64,7... | collective-permute-start | bytes 49160 | tf_op jit(solution)/shard_map/ppermute | solution.py:16
  206.4 5.1 %collective-permute-start.31 = (f32[18,1,128]{2,1,0:T(1,128)S(1)}, f32[18,1,128]{2,1,0:T(1,128)S(1)}, u32[]{:S(2)}, u32[]{:S(2)}) collective-permute-start(f32[18,1,128]{2,1,0:T(1,128)S(1)} %get-tuple-element.66), channel_id=1, source_target_pairs={{0,1},{1,2},{2,3},{3,4},{4,5},{5,6},{6,7},{8,9},{9,10},{10,11},{11... | collective-permute-start | bytes 27656 | tf_op jit(solution)/shard_map/ppermute | solution.py:16
  215.0 4.2 %collective-permute-start.33 = (f32[1,32,128]{2,1,0:T(8,128)S(1)}, f32[1,32,128]{2,1,0:T(8,128)S(1)}, u32[]{:S(2)}, u32[]{:S(2)}) collective-permute-start(f32[1,32,128]{2,1,0:T(8,128)S(1)} %get-tuple-element.74), channel_id=1, source_target_pairs={{0,8},{8,16},{16,24},{24,32},{32,40},{40,48},{48,56},{56,64},{64,7... | collective-permute-start | bytes 49160 | tf_op jit(solution)/shard_map/ppermute | solution.py:16
  222.0 4.8 %collective-permute-start.35 = (f32[18,1,128]{2,1,0:T(1,128)S(1)}, f32[18,1,128]{2,1,0:T(1,128)S(1)}, u32[]{:S(2)}, u32[]{:S(2)}) collective-permute-start(f32[18,1,128]{2,1,0:T(1,128)S(1)} %get-tuple-element.64), channel_id=1, source_target_pairs={{0,1},{1,2},{2,3},{3,4},{4,5},{5,6},{6,7},{8,9},{9,10},{10,11},{11... | collective-permute-start | bytes 27656 | tf_op jit(solution)/shard_map/ppermute | solution.py:16
  229.6 76.3 %psum.14 = f32[6]{0:T(128)S(1)} all-reduce(f32[6]{0:T(128)S(1)} %pad_maximum_fusion.78), channel_id=1, replica_groups=mesh['blk'=32,'span'=8] {'blk'}, use_global_device_ids=true, to_apply=%region_2.3 | all-reduce | flops 6 | bytes 48 | tf_op jit(solution)/shard_map/psum | solution.py:154
  305.9 16.6 %psum.15 = f32[6]{0:T(128)S(1)} all-reduce(f32[6]{0:T(128)S(1)} %psum.14), channel_id=1, replica_groups=mesh['blk'=32,'span'=8] {'span'}, use_global_device_ids=true, to_apply=%region_3.4 | all-reduce | flops 6 | bytes 48 | tf_op jit(solution)/shard_map/psum | solution.py:154
  322.8 52.2 %all-gather.2 = f32[1,1024,128]{2,1,0:T(8,128)S(1)} all-gather(f32[1,32,128]{2,1,0:T(8,128)S(1)} %slice.616), channel_id=4, replica_groups=mesh['blk'=32,'span'=8] {'blk'}, dimensions={1}, use_global_device_ids=true | all-gather | bytes 540672 | tf_op jit(solution)/shard_map/all_gather | solution.py:147
  (162 shorter events, 72.6 us)
Async XLA Ops:
  3.0 46.9 %collective-permute-start.1 = (f32[5,1,32,128]{3,0,2,1:T(8,128)}, f32[5,1,32,128]{3,0,2,1:T(8,128)S(1)}, u32[]{:S(2)}, u32[]{:S(2)}) collective-permute-start(f32[5,1,32,128]{3,0,2,1:T(8,128)} %get-tuple-element.59), channel_id=1, source_target_pairs={{0,8},{8,16},{16,24},{24,32},{32,40},{40,48},{48,56},{56,64},{64,7... | collective-permute-start | bytes 245768 | tf_op jit(solution)/shard_map/ppermute | solution.py:16
  6.4 44.0 %collective-permute-start = (f32[5,1,32,128]{3,0,2,1:T(8,128)}, f32[5,1,32,128]{3,0,2,1:T(8,128)S(1)}, u32[]{:S(2)}, u32[]{:S(2)}) collective-permute-start(f32[5,1,32,128]{3,0,2,1:T(8,128)} %get-tuple-element.58), channel_id=1, source_target_pairs={{8,0},{16,8},{24,16},{32,24},{40,32},{48,40},{56,48},{64,56},{72,6... | collective-permute-start | bytes 245768 | tf_op jit(solution)/shard_map/ppermute | solution.py:19
  9.6 37.7 %collective-permute-start.17 = (f32[1,32,128]{2,1,0:T(8,128)S(1)}, f32[1,32,128]{2,1,0:T(8,128)S(1)}, u32[]{:S(2)}, u32[]{:S(2)}) collective-permute-start(f32[1,32,128]{2,1,0:T(8,128)S(1)} %get-tuple-element.80), channel_id=1, source_target_pairs={{0,8},{8,16},{16,24},{24,32},{32,40},{40,48},{48,56},{56,64},{64,7... | collective-permute-start | bytes 49160 | tf_op jit(solution)/shard_map/ppermute | solution.py:16
  13.0 36.9 %collective-permute-start.16 = (f32[1,32,128]{2,1,0:T(8,128)S(1)}, f32[1,32,128]{2,1,0:T(8,128)S(1)}, u32[]{:S(2)}, u32[]{:S(2)}) collective-permute-start(f32[1,32,128]{2,1,0:T(8,128)S(1)} %get-tuple-element.81), channel_id=1, source_target_pairs={{8,0},{16,8},{24,16},{32,24},{40,32},{48,40},{56,48},{64,56},{72,6... | collective-permute-start | bytes 49160 | tf_op jit(solution)/shard_map/ppermute | solution.py:19
  15.5 49.9 %collective-permute-start.21 = (f32[1,32,128]{2,1,0:T(8,128)S(1)}, f32[1,32,128]{2,1,0:T(8,128)S(1)}, u32[]{:S(2)}, u32[]{:S(2)}) collective-permute-start(f32[1,32,128]{2,1,0:T(8,128)S(1)} %get-tuple-element.83), channel_id=1, source_target_pairs={{0,8},{8,16},{16,24},{24,32},{32,40},{40,48},{48,56},{56,64},{64,7... | collective-permute-start | bytes 49160 | tf_op jit(solution)/shard_map/ppermute | solution.py:16
  47.4 39.9 %collective-permute-start.20 = (f32[1,32,128]{2,1,0:T(8,128)S(1)}, f32[1,32,128]{2,1,0:T(8,128)S(1)}, u32[]{:S(2)}, u32[]{:S(2)}) collective-permute-start(f32[1,32,128]{2,1,0:T(8,128)S(1)} %get-tuple-element.82), channel_id=1, source_target_pairs={{8,0},{16,8},{24,16},{32,24},{40,32},{48,40},{56,48},{64,56},{72,6... | collective-permute-start | bytes 49160 | tf_op jit(solution)/shard_map/ppermute | solution.py:19
  51.8 8.1 %collective-permute-start.3 = (f32[5,10,1,128]{3,0,2,1:T(8,128)S(1)}, f32[5,10,1,128]{3,0,2,1:T(8,128)S(1)}, u32[]{:S(2)}, u32[]{:S(2)}) collective-permute-start(f32[5,10,1,128]{3,0,2,1:T(8,128)S(1)} %get-tuple-element.48), channel_id=1, source_target_pairs={{0,1},{1,2},{2,3},{3,4},{4,5},{5,6},{6,7},{8,9},{9,10},{10,11},{11... | collective-permute-start | bytes 76808 | tf_op jit(solution)/shard_map/ppermute | solution.py:16
  54.8 52.3 %collective-permute-start.18 = (f32[18,1,128]{2,1,0:T(1,128)S(1)}, f32[18,1,128]{2,1,0:T(1,128)S(1)}, u32[]{:S(2)}, u32[]{:S(2)}) collective-permute-start(f32[18,1,128]{2,1,0:T(1,128)S(1)} %get-tuple-element.71), channel_id=1, source_target_pairs={{1,0},{2,1},{3,2},{4,3},{5,4},{6,5},{7,6},{9,8},{10,9},{11,10},{12... | collective-permute-start | bytes 27656 | tf_op jit(solution)/shard_map/ppermute | solution.py:19
  56.2 54.9 %collective-permute-start.19 = (f32[18,1,128]{2,1,0:T(1,128)S(1)}, f32[18,1,128]{2,1,0:T(1,128)S(1)}, u32[]{:S(2)}, u32[]{:S(2)}) collective-permute-start(f32[18,1,128]{2,1,0:T(1,128)S(1)} %get-tuple-element.70), channel_id=1, source_target_pairs={{0,1},{1,2},{2,3},{3,4},{4,5},{5,6},{6,7},{8,9},{9,10},{10,11},{11... | collective-permute-start | bytes 27656 | tf_op jit(solution)/shard_map/ppermute | solution.py:16
  63.4 7.5 %collective-permute-start.4 = (f32[5,1,32,128]{3,0,2,1:T(8,128)S(1)}, f32[5,1,32,128]{3,0,2,1:T(8,128)S(1)}, u32[]{:S(2)}, u32[]{:S(2)}) collective-permute-start(f32[5,1,32,128]{3,0,2,1:T(8,128)S(1)} %get-tuple-element.57), channel_id=1, source_target_pairs={{8,0},{16,8},{24,16},{32,24},{40,32},{48,40},{56,48},{64,56},{72,6... | collective-permute-start | bytes 245768 | tf_op jit(solution)/shard_map/ppermute | solution.py:19
  65.4 7.5 %collective-permute-start.5 = (f32[5,1,32,128]{3,0,2,1:T(8,128)S(1)}, f32[5,1,32,128]{3,0,2,1:T(8,128)S(1)}, u32[]{:S(2)}, u32[]{:S(2)}) collective-permute-start(f32[5,1,32,128]{3,0,2,1:T(8,128)S(1)} %get-tuple-element.56), channel_id=1, source_target_pairs={{0,8},{8,16},{16,24},{24,32},{32,40},{40,48},{48,56},{56,64},{64,7... | collective-permute-start | bytes 245768 | tf_op jit(solution)/shard_map/ppermute | solution.py:16
  81.2 7.5 %collective-permute-start.8 = (f32[5,1,32,128]{3,0,2,1:T(8,128)S(1)}, f32[5,1,32,128]{3,0,2,1:T(8,128)S(1)}, u32[]{:S(2)}, u32[]{:S(2)}) collective-permute-start(f32[5,1,32,128]{3,0,2,1:T(8,128)S(1)} %get-tuple-element.55), channel_id=1, source_target_pairs={{8,0},{16,8},{24,16},{32,24},{40,32},{48,40},{56,48},{64,56},{72,6... | collective-permute-start | bytes 245768 | tf_op jit(solution)/shard_map/ppermute | solution.py:19
  83.1 7.4 %collective-permute-start.9 = (f32[5,1,32,128]{3,0,2,1:T(8,128)S(1)}, f32[5,1,32,128]{3,0,2,1:T(8,128)S(1)}, u32[]{:S(2)}, u32[]{:S(2)}) collective-permute-start(f32[5,1,32,128]{3,0,2,1:T(8,128)S(1)} %get-tuple-element.54), channel_id=1, source_target_pairs={{0,8},{8,16},{16,24},{24,32},{32,40},{40,48},{48,56},{56,64},{64,7... | collective-permute-start | bytes 245768 | tf_op jit(solution)/shard_map/ppermute | solution.py:16
  90.5 6.0 %collective-permute-start.10 = (f32[5,10,1,128]{3,0,2,1:T(8,128)S(1)}, f32[5,10,1,128]{3,0,2,1:T(8,128)S(1)}, u32[]{:S(2)}, u32[]{:S(2)}) collective-permute-start(f32[5,10,1,128]{3,0,2,1:T(8,128)S(1)} %get-tuple-element.45), channel_id=1, source_target_pairs={{1,0},{2,1},{3,2},{4,3},{5,4},{6,5},{7,6},{9,8},{10,9},{11,10},{12... | collective-permute-start | bytes 76808 | tf_op jit(solution)/shard_map/ppermute | solution.py:19
  91.8 10.4 %collective-permute-start.11 = (f32[5,10,1,128]{3,0,2,1:T(8,128)S(1)}, f32[5,10,1,128]{3,0,2,1:T(8,128)S(1)}, u32[]{:S(2)}, u32[]{:S(2)}) collective-permute-start(f32[5,10,1,128]{3,0,2,1:T(8,128)S(1)} %get-tuple-element.44), channel_id=1, source_target_pairs={{0,1},{1,2},{2,3},{3,4},{4,5},{5,6},{6,7},{8,9},{9,10},{10,11},{11... | collective-permute-start | bytes 76808 | tf_op jit(solution)/shard_map/ppermute | solution.py:16
  95.2 24.1 %collective-permute-start.22 = (f32[18,1,128]{2,1,0:T(1,128)S(1)}, f32[18,1,128]{2,1,0:T(1,128)S(1)}, u32[]{:S(2)}, u32[]{:S(2)}) collective-permute-start(f32[18,1,128]{2,1,0:T(1,128)S(1)} %get-tuple-element.73), channel_id=1, source_target_pairs={{1,0},{2,1},{3,2},{4,3},{5,4},{6,5},{7,6},{9,8},{10,9},{11,10},{12... | collective-permute-start | bytes 27656 | tf_op jit(solution)/shard_map/ppermute | solution.py:19
  96.5 22.8 %collective-permute-start.23 = (f32[18,1,128]{2,1,0:T(1,128)S(1)}, f32[18,1,128]{2,1,0:T(1,128)S(1)}, u32[]{:S(2)}, u32[]{:S(2)}) collective-permute-start(f32[18,1,128]{2,1,0:T(1,128)S(1)} %get-tuple-element.72), channel_id=1, source_target_pairs={{0,1},{1,2},{2,3},{3,4},{4,5},{5,6},{6,7},{8,9},{9,10},{10,11},{11... | collective-permute-start | bytes 27656 | tf_op jit(solution)/shard_map/ppermute | solution.py:16
  105.2 7.2 %collective-permute-start.12 = (f32[5,1,32,128]{3,0,2,1:T(8,128)S(1)}, f32[5,1,32,128]{3,0,2,1:T(8,128)S(1)}, u32[]{:S(2)}, u32[]{:S(2)}) collective-permute-start(f32[5,1,32,128]{3,0,2,1:T(8,128)S(1)} %get-tuple-element.53), channel_id=1, source_target_pairs={{8,0},{16,8},{24,16},{32,24},{40,32},{48,40},{56,48},{64,56},{72,6... | collective-permute-start | bytes 245768 | tf_op jit(solution)/shard_map/ppermute | solution.py:19
  107.2 7.5 %collective-permute-start.13 = (f32[5,1,32,128]{3,0,2,1:T(8,128)S(1)}, f32[5,1,32,128]{3,0,2,1:T(8,128)S(1)}, u32[]{:S(2)}, u32[]{:S(2)}) collective-permute-start(f32[5,1,32,128]{3,0,2,1:T(8,128)S(1)} %get-tuple-element.52), channel_id=1, source_target_pairs={{0,8},{8,16},{16,24},{24,32},{32,40},{40,48},{48,56},{56,64},{64,7... | collective-permute-start | bytes 245768 | tf_op jit(solution)/shard_map/ppermute | solution.py:16
  197.5 5.9 %collective-permute-start.28 = (f32[1,32,128]{2,1,0:T(8,128)S(1)}, f32[1,32,128]{2,1,0:T(8,128)S(1)}, u32[]{:S(2)}, u32[]{:S(2)}) collective-permute-start(f32[1,32,128]{2,1,0:T(8,128)S(1)} %get-tuple-element.77), channel_id=1, source_target_pairs={{8,0},{16,8},{24,16},{32,24},{40,32},{48,40},{56,48},{64,56},{72,6... | collective-permute-start | bytes 49160 | tf_op jit(solution)/shard_map/ppermute | solution.py:19
  205.1 6.4 %collective-permute-start.30 = (f32[18,1,128]{2,1,0:T(1,128)S(1)}, f32[18,1,128]{2,1,0:T(1,128)S(1)}, u32[]{:S(2)}, u32[]{:S(2)}) collective-permute-start(f32[18,1,128]{2,1,0:T(1,128)S(1)} %get-tuple-element.67), channel_id=1, source_target_pairs={{1,0},{2,1},{3,2},{4,3},{5,4},{6,5},{7,6},{9,8},{10,9},{11,10},{12... | collective-permute-start | bytes 27656 | tf_op jit(solution)/shard_map/ppermute | solution.py:19
  206.4 5.9 %collective-permute-start.31 = (f32[18,1,128]{2,1,0:T(1,128)S(1)}, f32[18,1,128]{2,1,0:T(1,128)S(1)}, u32[]{:S(2)}, u32[]{:S(2)}) collective-permute-start(f32[18,1,128]{2,1,0:T(1,128)S(1)} %get-tuple-element.66), channel_id=1, source_target_pairs={{0,1},{1,2},{2,3},{3,4},{4,5},{5,6},{6,7},{8,9},{9,10},{10,11},{11... | collective-permute-start | bytes 27656 | tf_op jit(solution)/shard_map/ppermute | solution.py:16
  213.1 6.2 %collective-permute-start.32 = (f32[1,32,128]{2,1,0:T(8,128)S(1)}, f32[1,32,128]{2,1,0:T(8,128)S(1)}, u32[]{:S(2)}, u32[]{:S(2)}) collective-permute-start(f32[1,32,128]{2,1,0:T(8,128)S(1)} %get-tuple-element.75), channel_id=1, source_target_pairs={{8,0},{16,8},{24,16},{32,24},{40,32},{48,40},{56,48},{64,56},{72,6... | collective-permute-start | bytes 49160 | tf_op jit(solution)/shard_map/ppermute | solution.py:19
  220.7 6.1 %collective-permute-start.34 = (f32[18,1,128]{2,1,0:T(1,128)S(1)}, f32[18,1,128]{2,1,0:T(1,128)S(1)}, u32[]{:S(2)}, u32[]{:S(2)}) collective-permute-start(f32[18,1,128]{2,1,0:T(1,128)S(1)} %get-tuple-element.65), channel_id=1, source_target_pairs={{1,0},{2,1},{3,2},{4,3},{5,4},{6,5},{7,6},{9,8},{10,9},{11,10},{12... | collective-permute-start | bytes 27656 | tf_op jit(solution)/shard_map/ppermute | solution.py:19
  (32 other events, 861.1 us)
